TPU v7x, 32 devices: a whole 2x2x4 slice. The times are simulated.
32 devices in a mesh: expert: 16 (over z, y, core), replica: 2 (over x).
Axes of the slice: x: 2, y: 2, z: 4, core: 2. Of those that a mesh axis runs over, the one named last changes fastest.
Arguments:
- tokens: bfloat16 [768, 7168], P('expert', 'replica'), may hold values from -18 to 18
- expert_ids: int32 [768, 8], P('expert'), may hold values from 0 to 15, all different within a row; in each aligned block of 48 rows (0 to 47, 48 to 95, ...) at most 48 rows name the same one
- route_weights: bfloat16 [768, 8], P('expert'), may hold values from 0.1 to 1.5
- gate_weight: bfloat16 [16, 7168, 1024], P('expert', 'replica'), may hold values from -0.0625 to 0.0625
- up_weight: bfloat16 [16, 7168, 1024], P('expert', 'replica'), may hold values from -0.0625 to 0.0625
- down_weight: bfloat16 [16, 1024, 7168], P('expert', None, 'replica'), may hold values from -0.1875 to 0.1875
- bin_edges: float32 [16], replicated, may hold values from 0 to 20, as said below
Outputs:
- mixed: bfloat16 [768, 7168], P('expert', 'replica')
- expert_load: float32 [16], P('expert')
Inputs may be any that keep to these rules, and one draw needn't show every extreme that they name: `expert_ids`: each row names 8 different experts; within the 48 rows of one index of expert no expert is named by more than 48 rows, a bound that some block reaches. `bin_edges`: strictly increasing and positive; the last edge is 20, above every token entry's magnitude.
All inputs are finite; a program needn't handle non-finite values.
Results may differ from a plain program's by a relative error of at most 0.019.
Values may be sent and summed in bfloat16 or wider, within the bound.
A program may use at most 128 MiB of HBM per device.

v0:
```python
import jax
import jax.numpy as jnp
from jax import lax
from jax.sharding import PartitionSpec as P

FINE = 8


clip_parts = 8


def above_counts(magnitude, levels):
    return lax.map(lambda level: jnp.sum((magnitude >= level).astype(jnp.int32), axis=0), levels)


def clip_scales(magnitude, edges, limit):
    coarse = above_counts(magnitude, edges)
    chosen = jnp.sum((coarse > limit).astype(jnp.int32), axis=0)
    places = jnp.arange(edges.shape[0], dtype=jnp.int32)
    upper = jnp.sum(
        jnp.where(
            places[:, None] == chosen[None, :], edges[:, None], jnp.zeros_like(edges)[:, None]
        ),
        axis=0,
    )
    lower = jnp.sum(
        jnp.where(
            places[:, None] == chosen[None, :] - 1, edges[:, None], jnp.zeros_like(edges)[:, None]
        ),
        axis=0,
    )
    fractions = jnp.arange(1, FINE + 1).astype(edges.dtype) / FINE
    levels = lower[None, :] + (upper - lower)[None, :] * fractions[:, None]
    levels = jnp.concatenate([levels[:-1], upper[None, :]], axis=0)
    refined = above_counts(magnitude, levels)
    picked = jnp.sum((refined > limit).astype(jnp.int32), axis=0)
    steps = jnp.arange(FINE, dtype=jnp.int32)
    return jnp.sum(
        jnp.where(steps[:, None] == picked[None, :], levels, jnp.zeros_like(levels)), axis=0
    )


def body(tokens, expert_ids, route_weights, gate_weight, up_weight, down_weight, bin_edges):
    experts = lax.axis_size("expert")
    replicas = lax.axis_size("replica")
    tok_rows, width = tokens.shape
    chosen_count = expert_ids.shape[1]
    hidden_units = gate_weight.shape[2]
    share = hidden_units // replicas
    capacity = min(tok_rows, tok_rows * chosen_count * 2 // experts)
    slots = experts * capacity
    flat_ids = expert_ids.reshape(-1)
    flat_weights = route_weights.reshape(-1).astype(jnp.float32)
    hits = (flat_ids[:, None] == jnp.arange(experts, dtype=jnp.int32)[None, :]).astype(jnp.int32)
    ranks = jnp.sum((jnp.cumsum(hits, axis=0) - hits) * hits, axis=1)
    position = flat_ids * capacity + ranks
    owner = jnp.arange(tok_rows * chosen_count, dtype=jnp.int32) // chosen_count
    placing = (position[:, None] == jnp.arange(slots, dtype=jnp.int32)[None, :]).astype(
        jnp.bfloat16
    )
    sourcing = (owner[:, None] == jnp.arange(tok_rows, dtype=jnp.int32)[None, :]).astype(
        jnp.bfloat16
    )
    dispatch_map = jnp.einsum(
        "as,at->st", placing, sourcing, preferred_element_type=jnp.float32
    ).astype(jnp.bfloat16)
    outgoing = jnp.dot(dispatch_map, tokens, preferred_element_type=jnp.float32).astype(
        jnp.bfloat16
    )
    arrived = lax.all_to_all(
        outgoing.reshape(experts, capacity, width),
        "expert",
        split_axis=0,
        concat_axis=0,
        tiled=True,
    )
    local_counts = jnp.sum(hits, axis=0).astype(jnp.float32)
    local_weighted = jnp.sum(hits.astype(jnp.float32) * flat_weights[:, None], axis=0)
    loads, weighted_loads = (
        lax.psum_scatter(local_counts, "expert", scatter_dimension=0, tiled=True),
        lax.psum_scatter(local_weighted, "expert", scatter_dimension=0, tiled=True),
    )
    limit = loads.astype(jnp.int32)[0] // clip_parts
    expert_load = weighted_loads / (tok_rows * chosen_count)
    rows = arrived.reshape(slots, width)
    scale = clip_scales(jnp.abs(rows), bin_edges, limit)
    quantized = (jnp.clip(rows.astype(jnp.float32), -scale, scale) / scale).astype(jnp.bfloat16)
    gate_fold = (gate_weight[0].astype(jnp.float32) * scale[:, None]).reshape(
        width, replicas, share
    )
    up_fold = (up_weight[0].astype(jnp.float32) * scale[:, None]).reshape(width, replicas, share)
    paired = (
        jnp.stack([gate_fold, up_fold], axis=2)
        .reshape(width, 2 * hidden_units)
        .astype(jnp.bfloat16)
    )
    partial_value = jnp.dot(quantized, paired, preferred_element_type=jnp.float32)
    mine = lax.psum_scatter(
        partial_value.astype(jnp.bfloat16), "replica", scatter_dimension=1, tiled=True
    ).astype(jnp.float32)
    hidden_piece = (jax.nn.silu(mine[:, :share]) * mine[:, share:]).astype(jnp.bfloat16)
    down_rows = down_weight[0]
    result = jnp.dot(
        lax.all_gather(hidden_piece, "replica", axis=1, tiled=True),
        down_rows,
        preferred_element_type=jnp.float32,
    )
    expert_out = result.astype(jnp.bfloat16).reshape(experts, capacity, width)
    returned = lax.all_to_all(
        expert_out, "expert", split_axis=0, concat_axis=0, tiled=True
    ).reshape(slots, width)
    weighted = sourcing * route_weights.reshape(-1)[:, None]
    combine_map = jnp.einsum(
        "at,as->ts", weighted, placing, preferred_element_type=jnp.float32
    ).astype(jnp.bfloat16)
    mixed = jnp.dot(combine_map, returned, preferred_element_type=jnp.float32).astype(jnp.bfloat16)
    return (mixed, expert_load)


def solution(mesh):
    return jax.shard_map(
        body,
        mesh=mesh,
        in_specs=(
            P("expert", "replica"),
            P("expert", None),
            P("expert", None),
            P("expert", "replica", None),
            P("expert", "replica", None),
            P("expert", None, "replica"),
            P(),
        ),
        out_specs=(P("expert", "replica"), P("expert")),
        check_vma=False,
    )
```

profile of v0, /device:TPU:13, one launch (start us, length us, event | category | flops | bytes accessed | tf_op | source)
XLA Modules:
  0.0 574.2 jit_solution(13624238369832537749)
XLA Ops:
  14.0 6.7 %all-to-all-start = ((bf16[16,48,3584]{2,1,0:T(8,128)(2,1)}), bf16[16,48,3584]{2,1,0:T(8,128)(2,1)}, u32[]{:S(2)}, u32[]{:S(2)}) async-start(bf16[16,48,3584]{2,1,0:T(8,128)(2,1)} %bitcast.39), calls=%async_computation | async-start | bytes 11010048 | tf_op jit(solution)/shard_map/all_to_all | solution.py:70
  21.0 136.7 %all-reduce.2 = (f32[16]{0:T(128)S(1)}, f32[16]{0:T(128)S(1)}) all-reduce(f32[16]{0:T(128)S(1)} %convert_element_type.125, f32[16]{0:T(128)S(1)} %fusion.28), channel_id=2, replica_groups=mesh['expert'=16,'replica'=2] {'expert'}, use_global_device_ids=true, to_apply=%region_7.8.clone | all-reduce | flops 32 | bytes 256
  160.4 11.1 %copy.25 = f32[1,3584,1024]{1,2,0:T(8,128)} copy(bf16[1,3584,1024]{2,1,0:T(8,128)(2,1)} %param.14) | data formatting | bytes 22020096 | tf_op jit(solution)/shard_map/convert_element_type | solution.py:88
  171.5 11.1 %copy.26 = f32[1,3584,1024]{1,2,0:T(8,128)} copy(bf16[1,3584,1024]{2,1,0:T(8,128)(2,1)} %param.15) | data formatting | bytes 22020096 | tf_op jit(solution)/shard_map/convert_element_type | solution.py:91
  182.5 6.1 %abs.6 = bf16[16,48,3584]{2,1,0:T(8,128)(2,1)} abs(bf16[16,48,3584]{2,1,0:T(8,128)(2,1)} %all-to-all-done) | non-fusion elementwise | flops 2752512 | bytes 11010048 | tf_op jit(solution)/shard_map/abs | solution.py:86
  188.6 88.1 %while.20 = (s32[]{:T(128)}, s32[16,3584]{1,0:T(8,128)S(1)}, bf16[768,3584]{1,0:T(8,128)(2,1)}, f32[16]{0:T(128)S(1)}, s32[]{:T(128)}, /*index=5*/s32[]{:T(128)}) while((s32[]{:T(128)}, s32[16,3584]{1,0:T(8,128)S(1)}, bf16[768,3584]{1,0:T(8,128)(2,1)}, f32[16]{0:T(128)S(1)}, s32[]{:T(128)}, /*index=5*/s32[]{:T(128)}) %tuple.51), condition=%wide.region_5.6_spmd, body=%wide.region_3.5_spmd.sunk | while | flops 11006466 | bytes 5576801 | solution.py:13
  189.2 4.6 convert_reduce_fusion.7
  194.7 4.6 convert_reduce_fusion.7
  200.2 4.6 convert_reduce_fusion.7
  205.7 4.6 convert_reduce_fusion.7
  211.2 4.6 convert_reduce_fusion.7
  216.7 4.6 convert_reduce_fusion.7
  222.2 4.6 convert_reduce_fusion.7
  227.7 4.6 convert_reduce_fusion.7
  233.2 4.6 convert_reduce_fusion.7
  238.7 4.6 convert_reduce_fusion.7
  244.2 4.6 convert_reduce_fusion.7
  249.7 4.6 convert_reduce_fusion.7
  255.2 4.6 convert_reduce_fusion.7
  260.8 4.6 convert_reduce_fusion.7
  266.3 4.6 convert_reduce_fusion.7
  271.8 4.6 convert_reduce_fusion.7
  277.1 35.7 %while.21 = (s32[]{:T(128)}, s32[8,3584]{1,0:T(8,128)S(1)}, bf16[768,3584]{1,0:T(8,128)(2,1)}, f32[8,3584]{1,0:T(8,128)S(1)}, s32[]{:T(128)}, /*index=5*/s32[]{:T(128)}) while((s32[]{:T(128)}, s32[8,3584]{1,0:T(8,128)S(1)}, bf16[768,3584]{1,0:T(8,128)(2,1)}, f32[8,3584]{1,0:T(8,128)S(1)}, s32[]{:T(128)}, /*index=5*/s32[]{:T(128)}) %tuple.50), condition=%wide.region_13.14_spmd, body=%wide.region_11.13_spmd.sunk | while | flops 11006466 | bytes 5619797 | solution.py:13
  312.9 10.4 %multiply_convert_fusion.1 = (bf16[3584,2,1,512]{0,3,2,1:T(8,128)(2,1)S(1)}, bf16[3584,2,1,512]{0,3,2,1:T(8,128)(2,1)S(1)}) fusion(f32[3584,2,1,512]{0,3,2,1:T(8,128)} %bitcast.37, f32[3584]{0:T(1024)S(1)} %select_reduce_fusion.2, f32[3584,2,1,512]{0,3,2,1:T(8,128)} %bitcast.38), kind=kLoop, calls=%fused_computation.7 | loop fusion | flops 14680064 | bytes 44054528 | tf_op jit(solution)/shard_map/convert.2
  323.3 6.3 %pad_maximum_fusion = bf16[3584,2,2,512]{0,3,2,1:T(8,128)(2,1)} fusion(bf16[3584,2,1,512]{0,3,2,1:T(8,128)(2,1)S(1)} %get-tuple-element.71, bf16[3584,2,1,512]{0,3,2,1:T(8,128)(2,1)S(1)} %get-tuple-element.70), kind=kLoop, calls=%fused_computation.5 | loop fusion | flops 7340032 | bytes 29360128 | tf_op jit(solution)/shard_map/stack | solution.py:93
  333.8 16.0 %convolution_convert_fusion.2 = bf16[768,2048]{1,0:T(8,128)(2,1)} fusion(bf16[768,3584]{1,0:T(8,128)(2,1)S(1)} %bitcast.42, bf16[3584,2048]{0,1:T(8,128)(2,1)} %bitcast.40), kind=kOutput, calls=%fused_computation.14 | convolution fusion | flops 11275862016 | bytes 23330816 | tf_op jit(solution)/shard_map/dot_general | solution.py:97
  350.1 43.7 %reduce-scatter.2.cloned.1.call-done = bf16[768,1024]{1,0:T(8,128)(2,1)} async-done(((bf16[768,2048]{1,0:T(8,128)(2,1)}), bf16[768,1024]{1,0:T(8,128)(2,1)}) %reduce-scatter.2.cloned.1.call-update) | async-done | bytes 1572880 | tf_op jit(solution)/shard_map/reduce_scatter | solution.py:98
  397.0 27.3 %all-gather.2.cloned.1.call-done = bf16[768,1024]{1,0:T(8,128)(2,1)} async-done(((bf16[768,512]{1,0:T(8,128)(2,1)}), bf16[768,1024]{1,0:T(8,128)(2,1)}) %all-gather.2.cloned.1.call-update) | async-done | bytes 1572880 | tf_op jit(solution)/shard_map/all_gather | solution.py:104
  424.3 10.1 %fusion.2 = bf16[768,3584]{1,0:T(8,128)(2,1)} fusion(bf16[768,1024]{1,0:T(8,128)(2,1)} %all-gather.2.cloned.1.call-done, bf16[1,1024,3584]{2,1,0:T(8,128)(2,1)} %param.16), kind=kOutput, calls=%fused_computation.11 | convolution fusion | flops 5639897088 | bytes 14417920 | tf_op jit(solution)/shard_map/dot_general | solution.py:103
  434.4 6.5 %all-to-all-start.1 = ((bf16[16,48,3584]{2,1,0:T(8,128)(2,1)}), bf16[16,48,3584]{2,1,0:T(8,128)(2,1)}, u32[]{:S(2)}, u32[]{:S(2)}) async-start(bf16[16,48,3584]{2,1,0:T(8,128)(2,1)} %bitcast.41), calls=%async_computation.2 | async-start | bytes 11010048 | tf_op jit(solution)/shard_map/all_to_all | solution.py:109
  442.9 118.6 %all-to-all-done.1 = bf16[16,48,3584]{2,1,0:T(8,128)(2,1)} async-done(((bf16[16,48,3584]{2,1,0:T(8,128)(2,1)}), bf16[16,48,3584]{2,1,0:T(8,128)(2,1)}, u32[]{:S(2)}, u32[]{:S(2)}) %all-to-all-start.1) | async-done | bytes 5505056 | tf_op jit(solution)/shard_map/all_to_all | solution.py:109
  561.5 4.7 convolution_convert_fusion.1
  (129 shorter events, 68.5 us)
Async XLA Ops:
  7.2 2.3 copy-start
  13.9 6.7 %copy-start.2 = (bf16[48,8]{0,1:T(8,128)(2,1)S(1)}, bf16[48,8]{0,1:T(8,128)(2,1)}, u32[]{:S(2)}) copy-start(bf16[48,8]{0,1:T(8,128)(2,1)} %param.13) | copy-start | bytes 2308
  13.9 143.8 %copy-start.4 = (u32[32]{0:T(128)S(1)}, u32[32]{0:T(128)}, u32[]{:S(2)}) copy-start(u32[32]{0:T(128)} %constant.77) | copy-start | bytes 388
  14.0 168.6 %all-to-all-start = ((bf16[16,48,3584]{2,1,0:T(8,128)(2,1)}), bf16[16,48,3584]{2,1,0:T(8,128)(2,1)}, u32[]{:S(2)}, u32[]{:S(2)}) async-start(bf16[16,48,3584]{2,1,0:T(8,128)(2,1)} %bitcast.39), calls=%async_computation | async-start | bytes 11010048 | tf_op jit(solution)/shard_map/all_to_all | solution.py:70
  20.6 373.1 %reduce-scatter.2.cloned.1.call-start = ((), (), s32[]{:S(2)}) async-start(), calls=%async_computation.3 | async-start | bytes 4718592 | tf_op jit(solution)/shard_map/reduce_scatter | solution.py:98
  182.5 6.1 %copy-start.3 = (f32[16]{0:T(128)S(1)}, f32[16]{0:T(128)}, u32[]{:S(2)}) copy-start(f32[16]{0:T(128)} %param.17) | copy-start | bytes 196
  349.8 74.5 %all-gather.2.cloned.1.call-start = ((), (), s32[]{:S(2)}) async-start(), calls=%async_computation.4 | async-start | bytes 2359296 | tf_op jit(solution)/shard_map/all_gather | solution.py:104
  434.4 127.1 %all-to-all-start.1 = ((bf16[16,48,3584]{2,1,0:T(8,128)(2,1)}), bf16[16,48,3584]{2,1,0:T(8,128)(2,1)}, u32[]{:S(2)}, u32[]{:S(2)}) async-start(bf16[16,48,3584]{2,1,0:T(8,128)(2,1)} %bitcast.41), calls=%async_computation.2 | async-start | bytes 11010048 | tf_op jit(solution)/shard_map/all_to_all | solution.py:109
  440.9 125.3 %copy-start.1 = (bf16[48,3584]{1,0:T(8,128)(2,1)S(1)}, bf16[48,3584]{1,0:T(8,128)(2,1)}, u32[]{:S(2)}) copy-start(bf16[48,3584]{1,0:T(8,128)(2,1)} %param.11) | copy-start | bytes 1032196
Sparse Core Ops, SparseCore 0:
  349.9 43.7 reduce-scatter.1
  397.1 27.1 all-gather.1
where the time goes:
time: 576 us; the launch traced here: 574 us
  waiting for transfers between devices  190 us (33%)
  other arithmetic  137 us (24%)
  blocking collectives  137 us (24%)
  local copies, waits for them, and re-layouts  44.6 us (8%)
  matrix products  35.3 us (6%)
  between operations  16.7 us (3%)
  starting transfers between devices  13.5 us (2%)
    unnamed x1, blocking collectives  137 us
    all_to_all x1, waiting for transfers between devices, body(): lax.all_to_all(expert_out, 'expert', split_axis=0, concat_axis=0, tiled=T...  119 us
    reduce_sum x24, other arithmetic, above_counts(): jnp.sum((magnitude >= level).astype(jnp.int32), axis=0)  105 us
    reduce_scatter x1, waiting for transfers between devices, body(): lax.psum_scatter(partial_value.astype(jnp.bfloat16), 'replica', scatter_d...  43.7 us
    all_gather x1, waiting for transfers between devices, body(): lax.all_gather(hidden_piece, 'replica', axis=1, tiled=True)  27.3 us
    dot_general x1, matrix products, body(): jnp.dot(quantized, paired, preferred_element_type=jnp.float32)  16 us
  transfers between devices with their start and end apart: 4, of which 3 were waited for; matrix products, arithmetic and copies ran while one was open for 4% of the time, Pallas kernels for 0%

commit v1 on v0

v1 whole, which is shorter than its diff:
```python
import functools

import jax
import jax.numpy as jnp
from jax import lax
from jax.experimental import pallas as pl
from jax.experimental.pallas import tpu as pltpu
from jax.sharding import PartitionSpec as P

FINE = 8
clip_parts = 8


def round_up(level):
    near = level.astype(jnp.bfloat16)
    wide = near.astype(jnp.float32)
    above = (wide * (1.0 + 0.75 * 2.0**-7)).astype(jnp.bfloat16)
    return jnp.where(wide < level, above.astype(jnp.float32), wide).astype(jnp.bfloat16)


def counts(magnitude_ref, level):
    rows, width = magnitude_ref.shape
    bound = jnp.broadcast_to(round_up(level), (16, width))
    one, zero = jnp.ones((16, width), jnp.bfloat16), jnp.zeros((16, width), jnp.bfloat16)

    def step(i, total):
        for k in range(8):
            block = magnitude_ref[pl.ds(pl.multiple_of(i * 128 + k * 16, 16), 16), :]
            total = total + jnp.where(block >= bound, one, zero)
        return total

    total = lax.fori_loop(0, rows // 128, step, zero)
    return jnp.sum(total.astype(jnp.float32), axis=0, keepdims=True)


def pick(index, values, other):
    result = jnp.full(index.shape, other, jnp.float32)
    for j, value in enumerate(values):
        result = jnp.where(index == j, value, result)
    return result


def clip_scale(magnitude_ref, edges, limit):
    width = magnitude_ref.shape[1]
    chosen = jnp.zeros((1, width), jnp.int32)
    step = 1
    while step * 2 < len(edges):
        step *= 2
    while step:
        passed = counts(magnitude_ref, pick(chosen + (step - 1), edges, edges[-1])) > limit
        chosen = jnp.where(passed, chosen + step, chosen)
        step //= 2
    upper = pick(chosen, edges, edges[-1])
    lower = pick(chosen - 1, edges, 0.0)
    picked = jnp.zeros((1, width), jnp.int32)

    def level(index):
        part = lower + (upper - lower) * ((index + 1).astype(jnp.float32) / FINE)
        return jnp.where(index >= FINE - 1, upper, part)

    step = FINE // 2
    while step:
        passed = counts(magnitude_ref, level(picked + (step - 1))) > limit
        picked = jnp.where(passed, picked + step, picked)
        step //= 2
    return level(picked)


def local_kernel(bins, edges_ref, x_ref, w_ref, gate_ref, up_ref, out_ref, magnitude, total):
    k = pl.program_id(0)
    named = w_ref[...] > 0.0
    limit = jnp.floor(jnp.sum(named.astype(jnp.float32)) / clip_parts)
    x = x_ref[...]
    magnitude[...] = jnp.where(named, jnp.abs(x.astype(jnp.float32)), 0.0).astype(jnp.bfloat16)
    edges = [edges_ref[j] for j in range(bins)]
    scale = clip_scale(magnitude, edges, limit).astype(jnp.bfloat16)
    x = jnp.minimum(jnp.maximum(x, -scale), scale)
    half = gate_ref.shape[1]

    @pl.when(k == 0)
    def _():
        total[...] = jnp.zeros_like(total)

    total[:, :half] += jnp.dot(x, gate_ref[...], preferred_element_type=jnp.float32)
    total[:, half:] += jnp.dot(x, up_ref[...], preferred_element_type=jnp.float32)

    @pl.when(k == pl.num_programs(0) - 1)
    def _():
        out_ref[...] = total[...].astype(out_ref.dtype)


def local_partial(x, w, gate, up, edges):
    rows, width = x.shape[0], gate.shape[0]
    hidden = gate.shape[1]
    chunk = 512 if width % 512 == 0 else 256
    return pl.pallas_call(
        functools.partial(local_kernel, edges.shape[0]),
        out_shape=jax.ShapeDtypeStruct((rows, 2 * hidden), jnp.bfloat16),
        grid=(width // chunk,),
        in_specs=[
            pl.BlockSpec(memory_space=pltpu.SMEM),
            pl.BlockSpec((rows, chunk), lambda k: (0, k)),
            pl.BlockSpec((rows, 1), lambda k: (0, 0)),
            pl.BlockSpec((chunk, hidden), lambda k: (k, 0)),
            pl.BlockSpec((chunk, hidden), lambda k: (k, 0)),
        ],
        out_specs=pl.BlockSpec((rows, 2 * hidden), lambda k: (0, 0)),
        scratch_shapes=[
            pltpu.VMEM((rows, chunk), jnp.bfloat16),
            pltpu.VMEM((rows, 2 * hidden), jnp.float32),
        ],
        compiler_params=pltpu.CompilerParams(vmem_limit_bytes=60 * 2**20),
    )(edges, x, w, gate, up)


def body(tokens, expert_ids, route_weights, gate_weight, up_weight, down_weight, bin_edges):
    experts = lax.axis_size("expert")
    me = lax.axis_index("expert")
    replicas = lax.axis_size("replica")
    tok_rows, width = tokens.shape
    top = expert_ids.shape[1]
    hidden_units = gate_weight.shape[2]
    share = hidden_units // replicas
    notes = jnp.concatenate([expert_ids.astype(jnp.bfloat16), route_weights], axis=1)
    notes = jnp.pad(notes, ((0, 0), (0, 128 - 2 * top)))
    x = lax.all_gather(jnp.concatenate([tokens, notes], axis=1), "expert", axis=0, tiled=True)
    ids = x[:, width : width + top].astype(jnp.int32)
    w = jnp.sum(
        jnp.where(ids == me, x[:, width + top : width + 2 * top].astype(jnp.float32), 0.0),
        axis=1,
        keepdims=True,
    )
    expert_load = (jnp.sum(w) / (tok_rows * top)).reshape(1)
    partial_value = local_partial(x, w, gate_weight[0], up_weight[0], bin_edges)
    paired = jnp.swapaxes(partial_value.reshape(-1, 2, replicas, share), 1, 2).reshape(
        -1, 2 * hidden_units
    )
    mine = lax.psum_scatter(paired, "replica", scatter_dimension=1, tiled=True).astype(jnp.float32)
    hidden_piece = (jax.nn.silu(mine[:, :share]) * mine[:, share:]).astype(jnp.bfloat16)
    hidden = lax.all_gather(hidden_piece, "replica", axis=1, tiled=True)
    result = jnp.dot(hidden, down_weight[0], preferred_element_type=jnp.float32)
    result = (w * result).astype(jnp.bfloat16)
    mixed = lax.psum_scatter(result, "expert", scatter_dimension=0, tiled=True)
    return (mixed, expert_load)


def solution(mesh):
    return jax.shard_map(
        body,
        mesh=mesh,
        in_specs=(
            P("expert", "replica"),
            P("expert", None),
            P("expert", None),
            P("expert", "replica", None),
            P("expert", "replica", None),
            P("expert", None, "replica"),
            P(),
        ),
        out_specs=(P("expert", "replica"), P("expert")),
        check_vma=False,
    )
```

time: 576 us -> 283 us (0.49)
  the two profiles are of different devices: /device:TPU:13 before, /device:TPU:0 now
where the time goes in v1:
time: 283 us; the launch traced here: 282 us
  waiting for transfers between devices  210 us (74%)
  Pallas kernels  26.3 us (9%)
  between operations  15.6 us (6%)
  local copies, waits for them, and re-layouts  12 us (4%)
  matrix products  10.3 us (4%)
  other arithmetic  7.99 us (3%)
    reduce_scatter x1, waiting for transfers between devices, body(): mixed = lax.psum_scatter(result, 'expert', scatter_dimension=0, tiled=True)  79.4 us
    all_gather x1, waiting for transfers between devices, body(): lax.all_gather(jnp.concatenate([tokens, notes], axis=1), 'expert', axis=0...  61 us
    reduce_scatter x1, waiting for transfers between devices, body(): lax.psum_scatter(paired, 'replica', scatter_dimension=1, tiled=True)  42.1 us
    all_gather x1, waiting for transfers between devices, body(): hidden = lax.all_gather(hidden_piece, 'replica', axis=1, tiled=True)  27.3 us
    pallas_call x1, Pallas kernels, local_partial(): pl.pallas_call(functools.partial(local_kernel, edges.shape[0]), out_shape...  26.3 us
    reshape x2, local copies, waits for them, and re-layouts, body(): partial_value.reshape(-1, 2, replicas, share)  10.9 us
    dot_general x1, matrix products, body(): result = jnp.dot(hidden, down_weight[0], preferred_element_type=jnp.float32)  10.3 us
  transfers between devices with their start and end apart: 4, of which 4 were waited for; matrix products, arithmetic and copies ran while one was open for 0% of the time, Pallas kernels for 0%

profile of v1, /device:TPU:0, one launch (start us, length us, event | category | flops | bytes accessed | tf_op | source)
XLA Modules:
  0.0 282.2 jit_solution(5196118966513636287)
XLA Ops:
  7.2 0.0 all-gather.3.cloned.1.call-start
  7.2 0.7 convert_element_type.20
  7.9 0.7 pad_maximum_fusion
  8.6 0.1 copy.15
  8.7 1.8 fusion.5
  10.4 0.0 all-gather.3.cloned.1.call-update
  10.5 0.0 reduce-scatter.3.cloned.1.call-start
  10.5 61.0 %all-gather.3.cloned.1.call-done.x_ref = bf16[768,3712]{1,0:T(8,128)(2,1)} async-done(((bf16[48,3712]{1,0:T(8,128)(2,1)}), bf16[768,3712]{1,0:T(8,128)(2,1)}) %all-gather.3.cloned.1.call-update) | async-done | bytes 5701648 | tf_op jit(solution)/shard_map/all_gather | solution.py:126
  71.5 1.9 fusion.3
  73.4 1.0 broadcast_in_dim.9.w_ref
  74.4 26.3 %shard_map.86 = bf16[768,2048]{1,0:T(8,128)(2,1)} custom-call(f32[16]{0:T(128)} %edges_ref.1, bf16[768,3712]{1,0:T(8,128)(2,1)} %all-gather.3.cloned.1.call-done.x_ref, f32[768,1]{1,0:T(8,128)} %broadcast_in_dim.9.w_ref, bf16[3584,1024]{1,0:T(8,128)(2,1)} %bitcast.11, bf16[3584,1024]{1,0:T(8,128)(2,1)} %bitcast.12), custom_call_target="tpu_custom_call" | custom-call | tf_op jit(solution)/shard_map/pallas_call | solution.py:96
  100.6 4.8 %reshape.14 = bf16[768,2,2,512]{3,2,1,0:T(2,128)(2,1)S(1)} reshape(bf16[768,2048]{1,0:T(8,128)(2,1)} %shard_map.86) | data formatting | bytes 6291456 | tf_op jit(solution)/shard_map/reshape | solution.py:135
  105.4 6.1 %copy.17 = bf16[768,2,2,512]{0,3,1,2:T(8,128)(2,1)} copy(bf16[768,2,2,512]{3,2,1,0:T(2,128)(2,1)S(1)} %reshape.14) | data formatting | bytes 6291456 | tf_op jit(solution)/shard_map/reshape | solution.py:135
  111.5 0.0 reduce-scatter.3.cloned.1.call-update
  111.6 0.0 all-gather.5.cloned.1.call-start
  111.6 42.1 %reduce-scatter.3.cloned.1.call-done = bf16[768,1024]{0,1:T(8,128)(2,1)} async-done(((bf16[768,2048]{0,1:T(8,128)(2,1)}), bf16[768,1024]{0,1:T(8,128)(2,1)}) %reduce-scatter.3.cloned.1.call-update) | async-done | bytes 1572880 | tf_op jit(solution)/shard_map/reduce_scatter | solution.py:138
  153.8 1.6 convert_element_type.23
  155.4 1.3 fusion.1
  156.8 0.0 all-gather.5.cloned.1.call-update
  156.8 0.0 reduce-scatter.5.cloned.1.call-start
  156.8 27.3 %all-gather.5.cloned.1.call-done = bf16[768,1024]{0,1:T(8,128)(2,1)} async-done(((bf16[768,512]{0,1:T(8,128)(2,1)}), bf16[768,1024]{0,1:T(8,128)(2,1)}) %all-gather.5.cloned.1.call-update) | async-done | bytes 1572880 | tf_op jit(solution)/shard_map/all_gather | solution.py:140
  184.1 10.3 %multiply_convert_fusion = bf16[768,3584]{1,0:T(8,128)(2,1)} fusion(bf16[768,1024]{0,1:T(8,128)(2,1)} %all-gather.5.cloned.1.call-done, bf16[1,1024,3584]{2,1,0:T(8,128)(2,1)} %param.12, f32[768]{0:T(1024)S(1)} %get-tuple-element.3), kind=kOutput, calls=%fused_computation | convolution fusion | flops 5642649600 | bytes 14420992 | tf_op jit(solution)/shard_map/dot_general | solution.py:141
  194.4 0.0 reduce-scatter.5.cloned.1.call-update
  195.1 79.4 %reduce-scatter.5.cloned.1.call-done = bf16[48,3584]{1,0:T(8,128)(2,1)} async-done(((bf16[768,3584]{1,0:T(8,128)(2,1)}), bf16[48,3584]{1,0:T(8,128)(2,1)}) %reduce-scatter.5.cloned.1.call-update) | async-done | bytes 344080 | tf_op jit(solution)/shard_map/reduce_scatter | solution.py:143
Async XLA Ops:
  7.2 64.4 %all-gather.3.cloned.1.call-start = ((), (), s32[]{:S(2)}) async-start(), calls=%async_computation.2 | async-start | bytes 6057984 | tf_op jit(solution)/shard_map/all_gather | solution.py:126
  10.5 143.3 %reduce-scatter.3.cloned.1.call-start = ((), (), s32[]{:S(2)}) async-start(), calls=%async_computation.3 | async-start | bytes 4718592 | tf_op jit(solution)/shard_map/reduce_scatter | solution.py:138
  111.6 72.6 %all-gather.5.cloned.1.call-start = ((), (), s32[]{:S(2)}) async-start(), calls=%async_computation.4 | async-start | bytes 2359296 | tf_op jit(solution)/shard_map/all_gather | solution.py:140
  156.8 117.7 %reduce-scatter.5.cloned.1.call-start = ((), (), s32[]{:S(2)}) async-start(), calls=%async_computation.5 | async-start | bytes 5849088 | tf_op jit(solution)/shard_map/reduce_scatter | solution.py:143
Sparse Core Ops, SparseCore 0:
  10.6 60.9 all-gather.2
  111.7 42.0 reduce-scatter.2
  156.9 27.1 all-gather.4
  194.6 79.8 reduce-scatter.4

commit v2 on v1

--- a/solution.py
+++ b/solution.py
@@ -113,6 +113,347 @@
     )(edges, x, w, gate, up)
 
 
+MESH = pl.DeviceIdType.MESH
+NOTE = 128
+KC = 4
+VMEM_MOST = 67043328
+
+
+def fused_kernel(
+    bins, top, x_hbm, gate_hbm, up_hbm, down_hbm, edges_ref, out_ref, load_ref,
+    xg, mag, wv, gu, down, sbuf, rbuf, own, hid, outb, sibr, scw, rcw, sccw, rccw,
+    load_sems, ring_send, ring_recv, sib_send, sib_recv, part_send, part_recv,
+    hid_send, hid_recv, pair_send, pair_recv, cw_send, cw_recv, ccw_send, ccw_recv,
+):
+    experts = lax.axis_size("expert")
+    me, r = lax.axis_index("expert"), lax.axis_index("replica")
+    chips = experts // 2
+    half_ring = chips // 2
+    c = lax.rem(me, 2)
+    chip = lax.div(me, 2)
+    odd, low = lax.rem(chip, 2), lax.div(chip, 2)
+    pos = (1 - odd) * low + odd * (chips - 1 - low)
+
+    def at(place):
+        place = lax.rem(place + chips, chips)
+        back = lax.div(place, half_ring)
+        number = (1 - back) * (2 * place) + back * (2 * (chips - 1 - place) + 1)
+        return (number * 2 + c, r)
+
+    right, left = at(pos + 1), at(pos - 1)
+    sibling = (chip * 2 + (1 - c), r)
+    partner = (me, 1 - r)
+
+    rows, wide = xg.shape
+    tok = rows // experts
+    width = wide - NOTE
+    share = hid.shape[1] // 2
+    tile = own.shape[2]
+    tiles = own.shape[0]
+    blocks = half_ring
+    brows = rows // blocks
+
+    own_load = pltpu.make_async_copy(
+        x_hbm, xg.at[pl.ds(pl.multiple_of(((chips - 1) * 2 + c) * tok, tok), tok), :], load_sems.at[0]
+    )
+    own_load.start()
+    weight_loads = [
+        pltpu.make_async_copy(gate_hbm, gu.at[0], load_sems.at[1]),
+        pltpu.make_async_copy(up_hbm, gu.at[1], load_sems.at[2]),
+        pltpu.make_async_copy(down_hbm, down, load_sems.at[3]),
+    ]
+    for copy in weight_loads:
+        copy.start()
+
+    barrier = pltpu.get_barrier_semaphore()
+    for other in (right, left, sibling, partner):
+        pl.semaphore_signal(barrier, inc=1, device_id=other, device_id_type=MESH)
+    pl.semaphore_wait(barrier, 4)
+    own_load.wait()
+
+    def slot(distance):
+        if distance == 0:
+            return chips - 1
+        if distance == half_ring or distance == -half_ring:
+            return chips - 2
+        return 2 * (distance - 1) if distance > 0 else 2 * (-distance - 1) + 1
+
+    def block(s, core, k):
+        step = width // KC
+        begin, size = (0, NOTE + step) if k == 0 else (NOTE + k * step, step)
+        start = pl.multiple_of((s * 2 + core) * tok, tok)
+        return xg.at[pl.ds(start, tok), pl.ds(begin, size)]
+
+    def ring_copy(distance, k, way):
+        nearer = slot(distance)
+        further = slot(distance + way)
+        return pltpu.make_async_remote_copy(
+            src_ref=block(nearer, c, k), dst_ref=block(further, c, k),
+            send_sem=ring_send.at[k, 0 if way > 0 else 1, abs(distance)],
+            recv_sem=ring_recv.at[k, further],
+            device_id=right if way > 0 else left, device_id_type=MESH,
+        )
+
+    def sib_copy(s, k):
+        return pltpu.make_async_remote_copy(
+            src_ref=block(s, c, k), dst_ref=block(s, c, k),
+            send_sem=sib_send.at[k, s], recv_sem=sib_recv.at[k, s],
+            device_id=sibling, device_id_type=MESH,
+        )
+
+    def sib_arrival(s, k):
+        return pltpu.make_async_remote_copy(
+            src_ref=block(s, 1 - c, k), dst_ref=block(s, 1 - c, k),
+            send_sem=sib_send.at[k, s], recv_sem=sib_recv.at[k, s],
+            device_id=sibling, device_id_type=MESH,
+        )
+
+    started = []
+    events = sorted((h + 2 * k, k, h) for k in range(KC) for h in range(half_ring + 1))
+    for _, k, h in events:
+        for way in (1, -1):
+            hops = half_ring if (way > 0) == (k % 2 == 0) else half_ring - 1
+            if h > hops:
+                continue
+            if h > 0:
+                ring_copy(way * (h - 1), k, way).wait_recv()
+            if h < hops:
+                copy = ring_copy(way * h, k, way)
+                copy.start()
+                started.append(copy)
+            if h > 0 or way > 0:
+                copy = sib_copy(slot(way * h), k)
+                copy.start()
+                started.append(copy)
+    for k in range(KC):
+        for s in range(chips):
+            sib_arrival(s, k).wait_recv()
+    for copy in started:
+        copy.wait_send()
+
+    lane = lax.broadcasted_iota(jnp.int32, (rows, NOTE), 1)
+    wv[...] = jnp.sum(
+        jnp.where(lane == me, xg[:, 0:NOTE].astype(jnp.float32), 0.0), axis=1, keepdims=True
+    )
+    load_ref[...] = jnp.full(load_ref.shape, jnp.sum(wv[...]) / (tok * top), jnp.float32)
+    limit = jnp.floor(jnp.sum((wv[...] > 0.0).astype(jnp.float32)) / clip_parts)
+    edges = [edges_ref[j] for j in range(bins)]
+    chunk = mag.shape[1]
+
+    def clip_step(k, carry):
+        columns = pl.ds(pl.multiple_of(NOTE + k * chunk, 128), chunk)
+        x = xg[:, columns]
+        mag[...] = jnp.where(wv[...] > 0.0, jnp.abs(x.astype(jnp.float32)), 0.0).astype(jnp.bfloat16)
+        scale = clip_scale(mag, edges, limit).astype(jnp.bfloat16)
+        xg[:, columns] = jnp.minimum(jnp.maximum(xg[:, columns], -scale), scale)
+        return carry
+
+    lax.fori_loop(0, width // chunk, clip_step, 0)
+
+    weight_loads[0].wait()
+    weight_loads[1].wait()
+    per = tiles // 2
+
+    def product(j, side):
+        begin = pl.multiple_of(side * share + lax.rem(j, per) * tile, 128)
+        return jnp.dot(
+            xg[:, NOTE:], gu[lax.div(j, per), :, pl.ds(begin, tile)],
+            preferred_element_type=jnp.float32,
+        )
+
+    def part_copy(j, i):
+        span = pl.ds(pl.multiple_of(i * brows, brows), brows)
+        return pltpu.make_async_remote_copy(
+            src_ref=sbuf.at[j, span, :], dst_ref=rbuf.at[j, span, :],
+            send_sem=part_send.at[j, i], recv_sem=part_recv.at[j, i],
+            device_id=partner, device_id_type=MESH,
+        )
+
+    def send_step(j, carry):
+        sbuf[j] = product(j, 1 - r).astype(jnp.bfloat16)
+        for i in range(blocks):
+            part_copy(j, i).start()
+        return carry
+
+    def keep_step(j, carry):
+        own[j] = product(j, r)
+        return carry
+
+    lax.fori_loop(0, tiles, send_step, 0)
+    lax.fori_loop(0, tiles, keep_step, 0)
+
+    def hid_copy(i, side):
+        place = hid.at[
+            pl.ds(pl.multiple_of(i * brows, brows), brows),
+            pl.ds(pl.multiple_of(side * share, 128), share),
+        ]
+        return pltpu.make_async_remote_copy(
+            src_ref=place, dst_ref=place, send_sem=hid_send.at[i], recv_sem=hid_recv.at[i],
+            device_id=partner, device_id_type=MESH,
+        )
+
+    def hidden_step(i, carry):
+        span = pl.ds(pl.multiple_of(i * brows, brows), brows)
+        for j in range(tiles):
+            part_copy(j, i).wait_recv()
+        for j in range(per):
+            gate = own[j, span, :] + rbuf[j, span, :].astype(jnp.float32)
+            up = own[j + per, span, :] + rbuf[j + per, span, :].astype(jnp.float32)
+            place = pl.ds(pl.multiple_of(r * share + j * tile, 128), tile)
+            hid[span, place] = (gate / (1.0 + jnp.exp(-gate)) * up).astype(jnp.bfloat16)
+        hid_copy(i, r).start()
+        return carry
+
+    lax.fori_loop(0, blocks, hidden_step, 0)
+
+    weight_loads[2].wait()
+    middle = width // 2
+
+    def pair_copy(s):
+        span = pl.ds(pl.multiple_of((s * 2 + (1 - c)) * tok, tok), tok)
+        return pltpu.make_async_remote_copy(
+            src_ref=outb.at[span, :], dst_ref=sibr.at[s],
+            send_sem=pair_send.at[s], recv_sem=pair_recv.at[s],
+            device_id=sibling, device_id_type=MESH,
+        )
+
+    def cw_copy(s):
+        return pltpu.make_async_remote_copy(
+            src_ref=scw.at[s], dst_ref=rcw.at[s], send_sem=cw_send.at[s], recv_sem=cw_recv.at[s],
+            device_id=right, device_id_type=MESH,
+        )
+
+    def ccw_copy(s):
+        return pltpu.make_async_remote_copy(
+            src_ref=sccw.at[s], dst_ref=rccw.at[s], send_sem=ccw_send.at[s], recv_sem=ccw_recv.at[s],
+            device_id=left, device_id_type=MESH,
+        )
+
+    def share_of(s, begin):
+        span = pl.ds(pl.multiple_of((s * 2 + c) * tok, tok), tok)
+        mine = outb[span, begin : begin + middle].astype(jnp.float32)
+        return mine + sibr[s, :, begin : begin + middle].astype(jnp.float32)
+
+    def ring_step(s, cw_slot, ccw_slot):
+        cw_copy(s - 1).wait_recv()
+        scw[s] = (share_of(cw_slot, 0) + rcw[s - 1].astype(jnp.float32)).astype(jnp.bfloat16)
+        cw_copy(s).start()
+        ccw_copy(s - 1).wait_recv()
+        sccw[s] = (share_of(ccw_slot, middle) + rccw[s - 1].astype(jnp.float32)).astype(jnp.bfloat16)
+        ccw_copy(s).start()
+
+    piece = 512 if width % 512 == 0 else 128
+
+    def down_step(i, carry):
+        span = pl.ds(pl.multiple_of(i * brows, brows), brows)
+        hid_copy(i, 1 - r).wait_recv()
+
+        def columns_step(n, carry):
+            columns = pl.ds(pl.multiple_of(n * piece, 128), piece)
+            result = jnp.dot(hid[span, :], down[:, columns], preferred_element_type=jnp.float32)
+            outb[span, columns] = (wv[span, :] * result).astype(jnp.bfloat16)
+            return carry
+
+        lax.fori_loop(0, width // piece, columns_step, 0)
+        pair_copy(2 * i).start()
+        pair_copy(2 * i + 1).start()
+        pair_copy(2 * i).wait_recv()
+        pair_copy(2 * i + 1).wait_recv()
+
+        @pl.when(i == 0)
+        def _():
+            scw[0] = share_of(0, 0).astype(jnp.bfloat16)
+            cw_copy(0).start()
+            sccw[0] = share_of(1, middle).astype(jnp.bfloat16)
+            ccw_copy(0).start()
+
+        @pl.when(i > 0)
+        def _():
+            ring_step(i, 2 * i, jnp.minimum(2 * i + 1, chips - 2))
+
+        return carry
+
+    lax.fori_loop(0, blocks, down_step, 0)
+    for s in range(half_ring, chips - 1):
+        back = 2 * (s - half_ring)
+        ring_step(s, chips - 3 - back, chips - 4 - back)
+    cw_copy(chips - 2).wait_recv()
+    out_ref[:, :middle] = (
+        share_of(chips - 1, 0) + rcw[chips - 2].astype(jnp.float32)
+    ).astype(out_ref.dtype)
+    ccw_copy(chips - 2).wait_recv()
+    out_ref[:, middle:] = (
+        share_of(chips - 1, middle) + rccw[chips - 2].astype(jnp.float32)
+    ).astype(out_ref.dtype)
+    for i in range(blocks):
+        for j in range(tiles):
+            part_copy(j, i).wait_send()
+        hid_copy(i, r).wait_send()
+    for s in range(chips):
+        pair_copy(s).wait_send()
+    for s in range(chips - 1):
+        cw_copy(s).wait_send()
+        ccw_copy(s).wait_send()
+
+
+def fused_scratch(experts, tok, width, hidden):
+    rows, chips = experts * tok, experts // 2
+    share = hidden // 2
+    tile = 256 if share % 256 == 0 else 128
+    tiles = 2 * share // tile
+    chunk = 512 if width % 512 == 0 else 128
+    bf, f32 = jnp.bfloat16, jnp.float32
+    ring = (chips - 1, tok, width // 2)
+    return [
+        ((rows, NOTE + width), bf), ((rows, chunk), bf), ((rows, 1), f32),
+        ((2, width, hidden), bf), ((hidden, width), bf),
+        ((tiles, rows, tile), bf), ((tiles, rows, tile), bf), ((tiles, rows, tile), f32),
+        ((rows, hidden), bf), ((rows, width), bf), ((chips, tok, width), bf),
+        (ring, bf), (ring, bf), (ring, bf), (ring, bf),
+    ]
+
+
+def fused_fits(experts, replicas, tok, width, hidden):
+    held = 0
+    for shape, dtype in fused_scratch(experts, tok, width, hidden):
+        size = jnp.dtype(dtype).itemsize
+        for n in shape[:-1] + (max(shape[-1], 128),):
+            size *= n
+        held += size
+    even = experts % 4 == 0 and replicas == 2 and tok % 16 == 0 and experts <= NOTE
+    return even and width % (KC * 128) == 0 and held < 0.9 * VMEM_MOST
+
+
+def fused(x, gate, up, down, edges, experts, top):
+    tok, wide = x.shape
+    width, hidden = gate.shape
+    chips = experts // 2
+    shapes = fused_scratch(experts, tok, width, hidden)
+    tiles, blocks = shapes[5][0][0], chips // 2
+    dma = pltpu.SemaphoreType.DMA
+    any_spec = pl.BlockSpec(memory_space=pl.ANY)
+    vmem = pl.BlockSpec(memory_space=pltpu.VMEM)
+    return pl.pallas_call(
+        functools.partial(fused_kernel, edges.shape[0], top),
+        out_shape=(
+            jax.ShapeDtypeStruct((tok, width), jnp.bfloat16),
+            jax.ShapeDtypeStruct((1, 128), jnp.float32),
+        ),
+        in_specs=[any_spec] * 4 + [pl.BlockSpec(memory_space=pltpu.SMEM)],
+        out_specs=(vmem, vmem),
+        scratch_shapes=[pltpu.VMEM(shape, dtype) for shape, dtype in shapes]
+        + [
+            dma((4,)), dma((KC, 2, blocks)), dma((KC, chips)), dma((KC, chips)), dma((KC, chips)),
+            dma((tiles, blocks)), dma((tiles, blocks)), dma((blocks,)), dma((blocks,)),
+            dma((chips,)), dma((chips,)), dma((chips - 1,)), dma((chips - 1,)),
+            dma((chips - 1,)), dma((chips - 1,)),
+        ],
+        compiler_params=pltpu.CompilerParams(
+            collective_id=0, has_side_effects=True, vmem_limit_bytes=VMEM_MOST
+        ),
+    )(x, gate, up, down, edges)
+
+
 def body(tokens, expert_ids, route_weights, gate_weight, up_weight, down_weight, bin_edges):
     experts = lax.axis_size("expert")
     me = lax.axis_index("expert")
@@ -121,6 +462,17 @@
     top = expert_ids.shape[1]
     hidden_units = gate_weight.shape[2]
     share = hidden_units // replicas
+    if fused_fits(experts, replicas, tok_rows, width, hidden_units):
+        numbers = jnp.arange(NOTE, dtype=jnp.int32)
+        notes = sum(
+            jnp.where(expert_ids[:, k : k + 1] == numbers, route_weights[:, k : k + 1], 0)
+            for k in range(top)
+        )
+        mixed, load = fused(
+            jnp.concatenate([notes.astype(jnp.bfloat16), tokens], axis=1),
+            gate_weight[0], up_weight[0], down_weight[0], bin_edges, experts, top,
+        )
+        return mixed, load[0, :1]
     notes = jnp.concatenate([expert_ids.astype(jnp.bfloat16), route_weights], axis=1)
     notes = jnp.pad(notes, ((0, 0), (0, 128 - 2 * top)))
     x = lax.all_gather(jnp.concatenate([tokens, notes], axis=1), "expert", axis=0, tiled=True)

time: 283 us -> 155 us (0.55)
  waiting for transfers between devices: 210 us -> 0 us
  Pallas kernels: 26.3 us -> 146 us
  between operations: 15.6 us -> 2.45 us
  matrix products: 10.3 us -> 0 us
  local copies, waits for them, and re-layouts: 12 us -> 3.7 us
  other arithmetic: 7.99 us -> 1.9 us
    reduce_scatter x2 -> x0, waiting for transfers between devices: 122 us -> none  [the longest x1 79.4 us: body(): mixed = lax.psum_scatter(result, 'expert', scatter_dimension=0, tiled=True)]
    pallas_call x1, Pallas kernels: 26.3 us -> 146 us  [fused(): pl.pallas_call(functools.partial(fused_kernel, edges.shape[0], top), out_...]
    all_gather x2 -> x0, waiting for transfers between devices: 88.3 us -> none  [the longest x1 61 us: body(): lax.all_gather(jnp.concatenate([tokens, notes], axis=1), 'expert', axis=0...]
    reshape x2 -> x0, local copies, waits for them, and re-layouts: 10.9 us -> none  [body(): partial_value.reshape(-1, 2, replicas, share)]
    dot_general x1 -> x0, matrix products: 10.3 us -> none  [body(): result = jnp.dot(hidden, down_weight[0], preferred_element_type=jnp.float32)]
    convert_element_type x3 -> x0, other arithmetic: 3.68 us -> none  [the longest x1 1.64 us: body(): lax.psum_scatter(paired, 'replica', scatter_dimension=1, tiled=True)]
  transfers between devices with their start and end apart: 4 -> 0, of which waited for: 4 -> 0; matrix products, arithmetic and copies ran while one was open for 0% -> 0% of each run, Pallas kernels for 0% -> 0%
where the time goes in v2:
time: 155 us; the launch traced here: 154 us
  Pallas kernels  146 us (94%)
  local copies, waits for them, and re-layouts  3.7 us (2%)
  between operations  2.45 us (2%)
  other arithmetic  1.9 us (1%)
    pallas_call x1, Pallas kernels, fused(): pl.pallas_call(functools.partial(fused_kernel, edges.shape[0], top), out_...  146 us

profile of v2, /device:TPU:0, one launch (start us, length us, event | category | flops | bytes accessed | tf_op | source)
XLA Modules:
  0.0 154.2 jit_solution(708745783010746974)
XLA Ops:
  0.6 1.0 slice_bitcast_fusion.15
  1.6 1.0 slice_bitcast_fusion.14
  2.6 0.2 fusion.8
  2.8 1.7 %pad_maximum_fusion.x_hbm = bf16[48,3712]{1,0:T(8,128)(2,1)} fusion(bf16[48,3584]{1,0:T(8,128)(2,1)} %param.7, bf16[48,128]{1,0:T(8,128)(2,1)S(1)} %fusion.8), kind=kLoop, calls=%fused_computation | loop fusion | flops 712704 | bytes 712704 | tf_op jit(solution)/shard_map/concatenate | solution.py:472
  4.5 146.2 %shard_map.86 = (bf16[48,3584]{1,0:T(8,128)(2,1)}, f32[1,128]{1,0:T(1,128)}) custom-call(bf16[48,3712]{1,0:T(8,128)(2,1)} %pad_maximum_fusion.x_hbm, bf16[3584,1024]{1,0:T(8,128)(2,1)} %bitcast.37, bf16[3584,1024]{1,0:T(8,128)(2,1)} %bitcast.38, bf16[1024,3584]{1,0:T(8,128)(2,1)} %bitcast.39, f32[16]{0:T(128)} %edges_ref.1), custom_call_target="tpu_custom_call" | custom-call | tf_op jit(solution)/shard_map/pallas_call | solution.py:436
  150.7 1.7 %copy.11 = bf16[48,3584]{1,0:T(8,128)(2,1)} copy(bf16[48,3584]{1,0:T(8,128)(2,1)} %get-tuple-element.24) | data formatting | bytes 688128

commit v3 on v2

--- a/solution.py
+++ b/solution.py
@@ -154,7 +154,7 @@
     brows = rows // blocks
 
     own_load = pltpu.make_async_copy(
-        x_hbm, xg.at[pl.ds(pl.multiple_of(((chips - 1) * 2 + c) * tok, tok), tok), :], load_sems.at[0]
+        x_hbm, xg.at[pl.ds(pl.multiple_of((2 + c) * tok, tok), tok), :], load_sems.at[0]
     )
     own_load.start()
     weight_loads = [
@@ -173,10 +173,10 @@
 
     def slot(distance):
         if distance == 0:
-            return chips - 1
-        if distance == half_ring or distance == -half_ring:
-            return chips - 2
-        return 2 * (distance - 1) if distance > 0 else 2 * (-distance - 1) + 1
+            return 1
+        if abs(distance) == half_ring:
+            return 0
+        return 2 * (half_ring - abs(distance)) + (0 if distance > 0 else 1)
 
     def block(s, core, k):
         step = width // KC
@@ -209,7 +209,7 @@
         )
 
     started = []
-    events = sorted((h + 2 * k, k, h) for k in range(KC) for h in range(half_ring + 1))
+    events = sorted((h + k, k, h) for k in range(KC) for h in range(half_ring + 1))
     for _, k, h in events:
         for way in (1, -1):
             hops = half_ring if (way > 0) == (k % 2 == 0) else half_ring - 1
@@ -254,10 +254,10 @@
     weight_loads[1].wait()
     per = tiles // 2
 
-    def product(j, side):
+    def product(j, side, span):
         begin = pl.multiple_of(side * share + lax.rem(j, per) * tile, 128)
         return jnp.dot(
-            xg[:, NOTE:], gu[lax.div(j, per), :, pl.ds(begin, tile)],
+            xg[span, NOTE:], gu[lax.div(j, per), :, pl.ds(begin, tile)],
             preferred_element_type=jnp.float32,
         )
 
@@ -268,19 +268,6 @@
             send_sem=part_send.at[j, i], recv_sem=part_recv.at[j, i],
             device_id=partner, device_id_type=MESH,
         )
-
-    def send_step(j, carry):
-        sbuf[j] = product(j, 1 - r).astype(jnp.bfloat16)
-        for i in range(blocks):
-            part_copy(j, i).start()
-        return carry
-
-    def keep_step(j, carry):
-        own[j] = product(j, r)
-        return carry
-
-    lax.fori_loop(0, tiles, send_step, 0)
-    lax.fori_loop(0, tiles, keep_step, 0)
 
     def hid_copy(i, side):
         place = hid.at[
@@ -292,8 +279,53 @@
             device_id=partner, device_id_type=MESH,
         )
 
-    def hidden_step(i, carry):
-        span = pl.ds(pl.multiple_of(i * brows, brows), brows)
+    middle = width // 2
+
+    def pair_copy(s):
+        span = pl.ds(pl.multiple_of((s * 2 + (1 - c)) * tok, tok), tok)
+        return pltpu.make_async_remote_copy(
+            src_ref=outb.at[span, :], dst_ref=sibr.at[s],
+            send_sem=pair_send.at[s], recv_sem=pair_recv.at[s],
+            device_id=sibling, device_id_type=MESH,
+        )
+
+    def sum_copy(sent, came, send_sem, recv_sem, s, first, target):
+        cols = pl.ds(first, middle) if s == 0 else pl.ds(0, width)
+        return pltpu.make_async_remote_copy(
+            src_ref=sent.at[s, :, cols], dst_ref=came.at[s, :, cols],
+            send_sem=send_sem.at[s], recv_sem=recv_sem.at[s],
+            device_id=target, device_id_type=MESH,
+        )
+
+    def cw_copy(s):
+        return sum_copy(scw, rcw, cw_send, cw_recv, s, 0, right)
+
+    def ccw_copy(s):
+        return sum_copy(sccw, rccw, ccw_send, ccw_recv, s, middle, left)
+
+    def share_of(s, begin, size):
+        span = pl.ds(pl.multiple_of((s * 2 + c) * tok, tok), tok)
+        mine = outb[span, begin : begin + size].astype(jnp.float32)
+        return mine + sibr[s, :, begin : begin + size].astype(jnp.float32)
+
+    def stage_send(i):
+        span = pl.ds(i * brows, brows)
+
+        def step(j, carry):
+            sbuf[j, span, :] = product(j, 1 - r, span).astype(jnp.bfloat16)
+            part_copy(j, i).start()
+            return carry
+
+        lax.fori_loop(0, tiles, step, 0)
+
+    def stage_hidden(i):
+        span = pl.ds(i * brows, brows)
+
+        def step(j, carry):
+            own[j, span, :] = product(j, r, span)
+            return carry
+
+        lax.fori_loop(0, tiles, step, 0)
         for j in range(tiles):
             part_copy(j, i).wait_recv()
         for j in range(per):
@@ -302,98 +334,64 @@
             place = pl.ds(pl.multiple_of(r * share + j * tile, 128), tile)
             hid[span, place] = (gate / (1.0 + jnp.exp(-gate)) * up).astype(jnp.bfloat16)
         hid_copy(i, r).start()
-        return carry
-
-    lax.fori_loop(0, blocks, hidden_step, 0)
-
-    weight_loads[2].wait()
-    middle = width // 2
-
-    def pair_copy(s):
-        span = pl.ds(pl.multiple_of((s * 2 + (1 - c)) * tok, tok), tok)
-        return pltpu.make_async_remote_copy(
-            src_ref=outb.at[span, :], dst_ref=sibr.at[s],
-            send_sem=pair_send.at[s], recv_sem=pair_recv.at[s],
-            device_id=sibling, device_id_type=MESH,
-        )
-
-    def cw_copy(s):
-        return pltpu.make_async_remote_copy(
-            src_ref=scw.at[s], dst_ref=rcw.at[s], send_sem=cw_send.at[s], recv_sem=cw_recv.at[s],
-            device_id=right, device_id_type=MESH,
-        )
-
-    def ccw_copy(s):
-        return pltpu.make_async_remote_copy(
-            src_ref=sccw.at[s], dst_ref=rccw.at[s], send_sem=ccw_send.at[s], recv_sem=ccw_recv.at[s],
-            device_id=left, device_id_type=MESH,
-        )
-
-    def share_of(s, begin):
-        span = pl.ds(pl.multiple_of((s * 2 + c) * tok, tok), tok)
-        mine = outb[span, begin : begin + middle].astype(jnp.float32)
-        return mine + sibr[s, :, begin : begin + middle].astype(jnp.float32)
-
-    def ring_step(s, cw_slot, ccw_slot):
-        cw_copy(s - 1).wait_recv()
-        scw[s] = (share_of(cw_slot, 0) + rcw[s - 1].astype(jnp.float32)).astype(jnp.bfloat16)
-        cw_copy(s).start()
-        ccw_copy(s - 1).wait_recv()
-        sccw[s] = (share_of(ccw_slot, middle) + rccw[s - 1].astype(jnp.float32)).astype(jnp.bfloat16)
-        ccw_copy(s).start()
 
     piece = 512 if width % 512 == 0 else 128
 
-    def down_step(i, carry):
-        span = pl.ds(pl.multiple_of(i * brows, brows), brows)
+    def stage_down(i):
+        span = pl.ds(i * brows, brows)
         hid_copy(i, 1 - r).wait_recv()
-
-        def columns_step(n, carry):
+        if i == 0:
+            weight_loads[2].wait()
+
+        def step(n, carry):
             columns = pl.ds(pl.multiple_of(n * piece, 128), piece)
             result = jnp.dot(hid[span, :], down[:, columns], preferred_element_type=jnp.float32)
             outb[span, columns] = (wv[span, :] * result).astype(jnp.bfloat16)
             return carry
 
-        lax.fori_loop(0, width // piece, columns_step, 0)
+        lax.fori_loop(0, width // piece, step, 0)
         pair_copy(2 * i).start()
         pair_copy(2 * i + 1).start()
         pair_copy(2 * i).wait_recv()
         pair_copy(2 * i + 1).wait_recv()
-
-        @pl.when(i == 0)
-        def _():
-            scw[0] = share_of(0, 0).astype(jnp.bfloat16)
-            cw_copy(0).start()
-            sccw[0] = share_of(1, middle).astype(jnp.bfloat16)
-            ccw_copy(0).start()
-
-        @pl.when(i > 0)
-        def _():
-            ring_step(i, 2 * i, jnp.minimum(2 * i + 1, chips - 2))
-
-        return carry
-
-    lax.fori_loop(0, blocks, down_step, 0)
-    for s in range(half_ring, chips - 1):
-        back = 2 * (s - half_ring)
-        ring_step(s, chips - 3 - back, chips - 4 - back)
-    cw_copy(chips - 2).wait_recv()
-    out_ref[:, :middle] = (
-        share_of(chips - 1, 0) + rcw[chips - 2].astype(jnp.float32)
-    ).astype(out_ref.dtype)
-    ccw_copy(chips - 2).wait_recv()
-    out_ref[:, middle:] = (
-        share_of(chips - 1, middle) + rccw[chips - 2].astype(jnp.float32)
-    ).astype(out_ref.dtype)
+        for sums, came, copy, s, first in (
+            (scw, rcw, cw_copy, 2 * i + 1 if i else 0, 0),
+            (sccw, rccw, ccw_copy, 2 * i, middle),
+        ):
+            if i:
+                copy(i - 1).wait_recv()
+            for begin in (0, middle):
+                cols = slice(begin, begin + middle)
+                if i == 0 and begin != first:
+                    continue
+                value = share_of(s, begin, middle)
+                if i > 1 or (i == 1 and begin == first):
+                    value = value + came[i - 1, :, cols].astype(jnp.float32)
+                sums[i, :, cols] = value.astype(jnp.bfloat16)
+            copy(i).start()
+
+    for t in range(blocks + 2):
+        if t < blocks:
+            stage_send(t)
+        if 1 <= t <= blocks:
+            stage_hidden(t - 1)
+        if t >= 2:
+            stage_down(t - 2)
+    last = blocks - 1
+    cw_copy(last).wait_recv()
+    ccw_copy(last).wait_recv()
+    for begin in (0, middle):
+        cols = slice(begin, begin + middle)
+        value = share_of(1, begin, middle) + rcw[last, :, cols].astype(jnp.float32)
+        out_ref[:, cols] = (value + rccw[last, :, cols].astype(jnp.float32)).astype(out_ref.dtype)
     for i in range(blocks):
         for j in range(tiles):
             part_copy(j, i).wait_send()
         hid_copy(i, r).wait_send()
+        cw_copy(i).wait_send()
+        ccw_copy(i).wait_send()
     for s in range(chips):
         pair_copy(s).wait_send()
-    for s in range(chips - 1):
-        cw_copy(s).wait_send()
-        ccw_copy(s).wait_send()
 
 
 def fused_scratch(experts, tok, width, hidden):
@@ -403,7 +401,7 @@
     tiles = 2 * share // tile
     chunk = 512 if width % 512 == 0 else 128
     bf, f32 = jnp.bfloat16, jnp.float32
-    ring = (chips - 1, tok, width // 2)
+    ring = (chips // 2, tok, width)
     return [
         ((rows, NOTE + width), bf), ((rows, chunk), bf), ((rows, 1), f32),
         ((2, width, hidden), bf), ((hidden, width), bf),
@@ -445,8 +443,8 @@
         + [
             dma((4,)), dma((KC, 2, blocks)), dma((KC, chips)), dma((KC, chips)), dma((KC, chips)),
             dma((tiles, blocks)), dma((tiles, blocks)), dma((blocks,)), dma((blocks,)),
-            dma((chips,)), dma((chips,)), dma((chips - 1,)), dma((chips - 1,)),
-            dma((chips - 1,)), dma((chips - 1,)),
+            dma((chips,)), dma((chips,)), dma((blocks,)), dma((blocks,)),
+            dma((blocks,)), dma((blocks,)),
         ],
         compiler_params=pltpu.CompilerParams(
             collective_id=0, has_side_effects=True, vmem_limit_bytes=VMEM_MOST

time: 155 us -> 134 us (0.86)
  Pallas kernels: 146 us -> 126 us
    pallas_call x1, Pallas kernels: 146 us -> 126 us  [fused(): pl.pallas_call(functools.partial(fused_kernel, edges.shape[0], top), out_...]
where the time goes in v3:
time: 134 us
  Pallas kernels  126 us (94%)
  local copies, waits for them, and re-layouts  3.7 us (3%)
  between operations  2.45 us (2%)
  other arithmetic  1.9 us (1%)
    pallas_call x1, Pallas kernels, fused(): pl.pallas_call(functools.partial(fused_kernel, edges.shape[0], top), out_...  126 us

profile of v3, /device:TPU:0, one launch (start us, length us, event | category | flops | bytes accessed | tf_op | source)
XLA Modules:
  0.0 134.2 jit_solution(7023905668846439102)
XLA Ops:
  0.6 1.0 slice_bitcast_fusion.15
  1.6 1.0 slice_bitcast_fusion.14
  2.6 0.2 fusion.8
  2.8 1.7 %pad_maximum_fusion.x_hbm = bf16[48,3712]{1,0:T(8,128)(2,1)} fusion(bf16[48,3584]{1,0:T(8,128)(2,1)} %param.7, bf16[48,128]{1,0:T(8,128)(2,1)S(1)} %fusion.8), kind=kLoop, calls=%fused_computation | loop fusion | flops 712704 | bytes 712704 | tf_op jit(solution)/shard_map/concatenate | solution.py:470
  4.5 126.1 %shard_map.86 = (bf16[48,3584]{1,0:T(8,128)(2,1)}, f32[1,128]{1,0:T(1,128)}) custom-call(bf16[48,3712]{1,0:T(8,128)(2,1)} %pad_maximum_fusion.x_hbm, bf16[3584,1024]{1,0:T(8,128)(2,1)} %bitcast.37, bf16[3584,1024]{1,0:T(8,128)(2,1)} %bitcast.38, bf16[1024,3584]{1,0:T(8,128)(2,1)} %bitcast.39, f32[16]{0:T(128)} %edges_ref.1), custom_call_target="tpu_custom_call" | custom-call | tf_op jit(solution)/shard_map/pallas_call | solution.py:434
  130.6 1.7 %copy.11 = bf16[48,3584]{1,0:T(8,128)(2,1)} copy(bf16[48,3584]{1,0:T(8,128)(2,1)} %get-tuple-element.24) | data formatting | bytes 688128

commit v4 on v3

--- a/solution.py
+++ b/solution.py
@@ -209,7 +209,7 @@
         )
 
     started = []
-    events = sorted((h + k, k, h) for k in range(KC) for h in range(half_ring + 1))
+    events = sorted((2 * h + k, k, h) for k in range(KC) for h in range(half_ring + 1))
     for _, k, h in events:
         for way in (1, -1):
             hops = half_ring if (way > 0) == (k % 2 == 0) else half_ring - 1

time: 134 us -> 130 us (0.970)
  Pallas kernels: 126 us -> 122 us
    pallas_call x1, Pallas kernels: 126 us -> 122 us  [fused(): pl.pallas_call(functools.partial(fused_kernel, edges.shape[0], top), out_...]
where the time goes in v4:
time: 130 us
  Pallas kernels  122 us (94%)
  local copies, waits for them, and re-layouts  3.7 us (3%)
  between operations  2.45 us (2%)
  other arithmetic  1.9 us (1%)
    pallas_call x1, Pallas kernels, fused(): pl.pallas_call(functools.partial(fused_kernel, edges.shape[0], top), out_...  122 us

profile of v4, /device:TPU:0, one launch (start us, length us, event | category | flops | bytes accessed | tf_op | source)
XLA Modules:
  0.0 129.8 jit_solution(17384655270122200461)
XLA Ops:
  0.6 1.0 slice_bitcast_fusion.15
  1.6 1.0 slice_bitcast_fusion.14
  2.6 0.2 fusion.8
  2.8 1.7 %pad_maximum_fusion.x_hbm = bf16[48,3712]{1,0:T(8,128)(2,1)} fusion(bf16[48,3584]{1,0:T(8,128)(2,1)} %param.7, bf16[48,128]{1,0:T(8,128)(2,1)S(1)} %fusion.8), kind=kLoop, calls=%fused_computation | loop fusion | flops 712704 | bytes 712704 | tf_op jit(solution)/shard_map/concatenate | solution.py:470
  4.5 121.7 %shard_map.86 = (bf16[48,3584]{1,0:T(8,128)(2,1)}, f32[1,128]{1,0:T(1,128)}) custom-call(bf16[48,3712]{1,0:T(8,128)(2,1)} %pad_maximum_fusion.x_hbm, bf16[3584,1024]{1,0:T(8,128)(2,1)} %bitcast.37, bf16[3584,1024]{1,0:T(8,128)(2,1)} %bitcast.38, bf16[1024,3584]{1,0:T(8,128)(2,1)} %bitcast.39, f32[16]{0:T(128)} %edges_ref.1), custom_call_target="tpu_custom_call" | custom-call | tf_op jit(solution)/shard_map/pallas_call | solution.py:434
  126.2 1.7 %copy.11 = bf16[48,3584]{1,0:T(8,128)(2,1)} copy(bf16[48,3584]{1,0:T(8,128)(2,1)} %get-tuple-element.24) | data formatting | bytes 688128
